TPU v7x, 256 devices: a whole 4x4x8 slice. The times are simulated.
256 devices in a mesh: side: 2 (over x_hi), row: 32 (over y, z), col: 4 (over x_lo, core).
Axes of the slice: x: 4 (x_hi: 2, x_lo: 2; x = x_hi * 2 + x_lo), y: 4, z: 8, core: 2. Of those that a mesh axis runs over, the one named last changes fastest.
Arguments:
- old_vectors: bfloat16 [2, 32768, 16384], P('side', 'row', 'col'), may hold values from -6 to 6
- reflectors: bfloat16 [2, 2, 32768, 512], P('side', None, 'row', 'col'), may hold values from -0.0625 to 0.0625
- triangles: float32 [2, 2, 512, 512], P('side'), may hold values from -0.25 to 0.25
- pole_sq: float32 [32768], replicated, may hold values from 1 to 65536, as said below
- coupling: float32 [32768], replicated, may hold values from -1 to 1
- deflated: int32 [32768], replicated, may hold values 0 or 1
- pole_order: int32 [32768], replicated, may hold values from 0 to 32767, each once
- anchors: int32 [1024], replicated, may hold values from 0 to 32766, as said below
- root_fraction: float32 [1024], replicated, may hold values from 0.2 to 0.8
Outputs:
- vectors: bfloat16 [2, 1024, 32768], P('side', 'col', 'row')
Inputs may be any that keep to these rules, and one draw needn't show every extreme that they name: `pole_sq`: strictly increasing; successive entries differ by 0.5 or more. `anchors`: distinct entries.
All inputs are finite; a program needn't handle non-finite values.
Results may differ from a plain program's by a relative error of at most 0.014.
Values may be sent and summed in bfloat16 or wider, within the bound.
A program may use at most 128 MiB of HBM per device.

v0:
```python
import jax
import jax.numpy as jnp
from jax import lax
from jax.sharding import PartitionSpec as P


def secular_columns(col_sq, col_coupling, col_live, weight, anchor_sq, pole_gap, root_fraction):
    denom = col_sq[:, None] - anchor_sq[None, :] - root_fraction[None, :] * pole_gap[None, :]
    return (col_live * col_coupling * weight)[:, None] / denom


def per_device(
    old_vectors,
    reflectors,
    triangles,
    pole_sq,
    coupling,
    deflated,
    pole_order,
    anchors,
    root_fraction,
):
    side_index = lax.axis_index("side")
    row_index = lax.axis_index("row")
    col_index = lax.axis_index("col")
    half_rows = lax.axis_size("row") // 2
    col_count = lax.axis_size("col")
    old_block = old_vectors[0]
    col_width = old_block.shape[1]
    order_size = pole_sq.shape[0]
    triplets = anchors.shape[0]
    local_triplets = triplets // col_count
    first_column = row_index // half_rows * (order_size // 2) + col_index * col_width
    columns = first_column + jnp.arange(col_width, dtype=jnp.int32)
    position = (
        jnp.zeros((order_size,), jnp.int32)
        .at[pole_order]
        .set(jnp.arange(order_size, dtype=jnp.int32))
    )
    sorted_pos = lax.dynamic_slice_in_dim(position, first_column, col_width)
    col_sq = pole_sq[sorted_pos]
    col_coupling = coupling[sorted_pos]
    col_live = (1 - deflated[sorted_pos]).astype(jnp.float32)
    weight = jnp.where(side_index == 0, jnp.ones_like(col_sq), jnp.sqrt(col_sq))
    anchor_sq = pole_sq[anchors]
    pole_gap = pole_sq[anchors + 1] - anchor_sq
    dead_triplet = deflated[anchors] == 1
    target = pole_order[anchors]
    secular = secular_columns(
        col_sq, col_coupling, col_live, weight, anchor_sq, pole_gap, root_fraction
    )
    onehot = (columns[:, None] == target[None, :]).astype(jnp.float32)
    mixing = jnp.where(dead_triplet[None, :], onehot, secular).astype(jnp.bfloat16)
    share_size = col_width // half_rows
    slice_part = lax.dynamic_slice_in_dim(
        secular, row_index % half_rows * share_size, share_size, 0
    )
    squares = lax.psum(jnp.sum(slice_part * slice_part, axis=0), ("row", "col"))
    col_scale = jnp.where(dead_triplet, jnp.ones_like(squares), 1.0 / jnp.sqrt(squares + 1e-06))
    merged = lax.psum_scatter(
        jnp.einsum("ck,rc->kr", mixing, old_block, preferred_element_type=jnp.float32).astype(
            jnp.bfloat16
        ),
        "col",
        scatter_dimension=0,
        tiled=True,
    ).astype(jnp.float32)
    my_scale = lax.dynamic_slice_in_dim(col_scale, col_index * local_triplets, local_triplets)
    vectors = merged * my_scale[:, None]
    panel_local = reflectors[0]
    panels = panel_local.shape[0]
    upper_tri = jnp.triu(triangles[0])
    highest = lax.Precision.HIGHEST
    for panel_index in reversed(range(panels)):
        panel_rows = panel_local[panel_index]
        current = vectors
        current_low = current.astype(jnp.bfloat16)
        projected = jnp.dot(
            current_low,
            lax.all_gather(panel_rows, "col", axis=1, tiled=True),
            preferred_element_type=jnp.float32,
        )
        projected = lax.psum(projected.astype(jnp.bfloat16), "row").astype(jnp.float32)
        coefficients = jnp.dot(projected, upper_tri[panel_index].T, precision=highest).astype(
            jnp.bfloat16
        )
        vectors = current - jnp.dot(
            coefficients,
            lax.all_gather(panel_rows, "col", axis=1, tiled=True).T,
            preferred_element_type=jnp.float32,
        )
    return vectors.astype(jnp.bfloat16)[None]


def solution(mesh):
    in_specs = (
        P("side", "row", "col"),
        P("side", None, "row", "col"),
        P("side", None, None, None),
        P(),
        P(),
        P(),
        P(),
        P(),
        P(),
    )
    out_specs = P("side", "col", "row")
    return jax.shard_map(
        per_device, mesh=mesh, in_specs=in_specs, out_specs=out_specs, check_vma=False
    )
```

profile of v0, /device:TPU:2, one launch (start us, length us, event | category | flops | bytes accessed | tf_op | source)
XLA Modules:
  0.0 883.1 jit_solution(16158088718118967877)
XLA Ops:
  6.5 0.0 copy-start
  6.5 0.0 all-gather.5.cloned.1.call-start
  6.5 1.9 fusion.23
  8.4 0.0 all-gather.5.cloned.1.call-update
  8.4 0.0 reduce-scatter.2.cloned.1.call-start
  8.5 0.9 compare_select_fusion
  9.5 120.1 %scatter_custom_fusion = s32[32768]{0:T(1024)S(1)} fusion(s32[32768]{0:T(1024)S(1)} %compare_select_fusion, s32[32768]{0:T(1024)S(1)} %iota.24, s32[]{:T(128)} %constant.23.clone.1), kind=kCustom, calls=%fused_computation.38 | custom fusion | bytes 131076 | tf_op jit(solution)/shard_map/scatter | solution.py:38
  129.6 0.0 copy-start.4
  129.6 0.0 copy-start.1
  129.6 19.5 %gather_fusion.2 = s32[4096]{0:T(1024)S(1)} fusion(s32[32768]{0:T(1024)} %param.14, s32[4096]{0:T(1024)S(1)} %fusion.20), kind=kCustom, calls=%fused_computation.2 | custom fusion | bytes 49152 | tf_op jit(solution)/shard_map/gather | solution.py:43
  149.2 0.0 copy-done
  149.2 0.0 copy-start.3
  149.2 0.0 copy-start.2
  149.2 23.0 %gather_fusion.4 = f32[4096]{0:T(1024)S(1)} fusion(f32[32768]{0:T(1024)S(1)} %copy-done, s32[4096]{0:T(1024)S(1)} %fusion.20), kind=kCustom, calls=%fused_computation.4 | custom fusion | bytes 49152 | tf_op jit(solution)/shard_map/gather | solution.py:41
  172.2 0.0 copy-done.4
  172.3 0.0 copy-start.5
  172.3 6.2 gather_fusion.5
  178.4 0.0 copy-done.1
  178.4 6.2 gather_fusion
  184.6 0.0 copy-done.3
  184.6 6.2 gather_fusion.1
  190.8 0.0 copy-done.2
  190.8 23.0 %gather_fusion.3 = f32[4096]{0:T(1024)S(1)} fusion(f32[32768]{0:T(1024)S(1)} %copy-done.2, s32[4096]{0:T(1024)S(1)} %fusion.20), kind=kCustom, calls=%fused_computation.3 | custom fusion | bytes 49152 | tf_op jit(solution)/shard_map/gather | solution.py:42
  213.8 6.2 gather_fusion.6
  220.0 6.5 subtract_divide_fusion
  226.5 1.3 multiply_reduce_fusion
  227.8 278.5 %psum.21 = f32[1024]{0:T(1024)S(1)} all-reduce(f32[1024]{0:T(1024)S(1)} %multiply_reduce_fusion), channel_id=1, replica_groups=mesh['side'=2,'row'=32,'col'=4] {'row','col'}, use_global_device_ids=true, to_apply=%region_3.4 | all-reduce | flops 1024 | bytes 8192 | tf_op jit(solution)/shard_map/psum | solution.py:58
  506.3 15.3 %fusion.5 = bf16[1024,1024]{1,0:T(8,128)(2,1)} fusion(bf16[1,1024,4096]{2,1,0:T(8,128)(2,1)} %param.9, s32[1024]{0:T(1024)S(1)} %gather_fusion.1, s32[4096]{0:T(1024)S(1)} %iota_add_fusion, pred[1024]{0:T(1024)(128)(4,1)S(1)} %get-tuple-element.6, f32[1024]{0:T(1024)S(1)} %subtract_multiply_fusion, f32[1024]{0:T(1024)S(1)} %gather_fusion.5, ...), kind=kOutput, calls=%fused_computation.16 | convolution fusion | flops 8620343296 | bytes 10548224 | tf_op jit(solution)/shard_map/ck,rc->kr/dot_general | solution.py:61
  521.7 0.0 reduce-scatter.2.cloned.1.call-update
  521.7 0.0 all-reduce.3.cloned.1.call-start
  521.8 0.1 dynamic_slice.11
  521.8 28.4 %reduce-scatter.2.cloned.1.call-done = bf16[256,1024]{1,0:T(8,128)(2,1)} async-done(((bf16[1024,1024]{1,0:T(8,128)(2,1)}), bf16[256,1024]{1,0:T(8,128)(2,1)}) %reduce-scatter.2.cloned.1.call-update) | async-done | bytes 524304 | tf_op jit(solution)/shard_map/reduce_scatter | solution.py:60
  550.3 2.6 convolution_convert_fusion.3
  552.9 0.0 all-reduce.3.cloned.1.call-update
  552.9 0.0 all-gather.7.cloned.1.call-start
  552.9 0.5 all-gather.7.cloned.1.call-update
  553.5 0.3 all-reduce.5.cloned.1.call-start
  553.7 0.2 iota_compare_fusion
  554.0 2.0 bitcast_select_fusion
  555.9 145.1 %all-reduce.3.cloned.1.call-done = bf16[256,512]{1,0:T(8,128)(2,1)} async-done(((bf16[256,512]{1,0:T(8,128)(2,1)}), bf16[256,512]{1,0:T(8,128)(2,1)}) %all-reduce.3.cloned.1.call-update) | async-done | bytes 262160 | tf_op jit(solution)/shard_map/psum | solution.py:83
  701.0 1.6 convolution_convert_fusion.2
  702.6 1.8 convolution_subtract_fusion.1
  704.5 18.7 %all-gather.7.cloned.1.call-done = bf16[1,1,1024,512]{3,2,1,0:T(8,128)(2,1)} async-done(((bf16[1,1,1024,128]{3,2,1,0:T(8,128)(2,1)}), bf16[1,1,1024,512]{3,2,1,0:T(8,128)(2,1)}) %all-gather.7.cloned.1.call-update) | async-done | bytes 1048592 | tf_op jit(solution)/shard_map/all_gather | solution.py:80
  723.1 2.4 convolution_convert_fusion.1
  725.5 0.0 all-reduce.5.cloned.1.call-update
  725.5 146.9 %all-reduce.5.cloned.1.call-done = bf16[256,512]{1,0:T(8,128)(2,1)} async-done(((bf16[256,512]{1,0:T(8,128)(2,1)}), bf16[256,512]{1,0:T(8,128)(2,1)}) %all-reduce.5.cloned.1.call-update) | async-done | bytes 262160 | tf_op jit(solution)/shard_map/psum | solution.py:83
  872.4 1.6 convolution_convert_fusion
  874.1 2.5 fusion.9
  (10 shorter events, 0.1 us)
Async XLA Ops:
  6.5 142.6 %copy-start = (f32[32768]{0:T(1024)S(1)}, f32[32768]{0:T(1024)}, u32[]{:S(2)}) copy-start(f32[32768]{0:T(1024)} %param.12) | copy-start | bytes 393220
  6.5 515.3 %all-gather.5.cloned.1.call-start = ((), (), s32[]{:S(2)}) async-start(), calls=%async_computation.4 | async-start | bytes 1310720 | tf_op jit(solution)/shard_map/all_gather | solution.py:80
  8.4 541.8 %reduce-scatter.2.cloned.1.call-start = ((), (), s32[]{:S(2)}) async-start(), calls=%async_computation.1 | async-start | bytes 2621440 | tf_op jit(solution)/shard_map/reduce_scatter | solution.py:60
  129.6 42.6 %copy-start.4 = (s32[1024]{0:T(1024)S(1)}, s32[1024]{0:T(1024)}, u32[]{:S(2)}) copy-start(s32[1024]{0:T(1024)} %param.16) | copy-start | bytes 12292
  129.6 48.8 %copy-start.1 = (s32[32768]{0:T(1024)S(1)}, s32[32768]{0:T(1024)}, u32[]{:S(2)}) copy-start(s32[32768]{0:T(1024)} %param.14) | copy-start | bytes 393220
  149.2 35.4 %copy-start.3 = (s32[32768]{0:T(1024)S(1)}, s32[32768]{0:T(1024)}, u32[]{:S(2)}) copy-start(s32[32768]{0:T(1024)} %param.15) | copy-start | bytes 393220
  149.2 41.6 %copy-start.2 = (f32[32768]{0:T(1024)S(1)}, f32[32768]{0:T(1024)}, u32[]{:S(2)}) copy-start(f32[32768]{0:T(1024)} %param.13) | copy-start | bytes 393220
  172.3 47.7 %copy-start.5 = (f32[1024]{0:T(1024)S(1)}, f32[1024]{0:T(1024)}, u32[]{:S(2)}) copy-start(f32[1024]{0:T(1024)} %param.17) | copy-start | bytes 12292
  521.7 179.3 %all-reduce.3.cloned.1.call-start = ((), (), s32[]{:S(2)}) async-start(), calls=%async_computation.2 | async-start | bytes 524288 | tf_op jit(solution)/shard_map/psum | solution.py:83
  552.9 170.3 %all-gather.7.cloned.1.call-start = ((), (), s32[]{:S(2)}) async-start(), calls=%async_computation.5 | async-start | bytes 1310720 | tf_op jit(solution)/shard_map/all_gather | solution.py:80
  553.5 319.0 %all-reduce.5.cloned.1.call-start = ((), (), s32[]{:S(2)}) async-start(), calls=%async_computation.3 | async-start | bytes 524288 | tf_op jit(solution)/shard_map/psum | solution.py:83
Sparse Core Ops, SparseCore 0:
  9.2 26.2 all-gather.4
  521.8 28.4 reduce-scatter.1
  554.1 146.8 all-reduce.2
  702.8 20.2 all-gather.6
  726.8 145.5 all-reduce.4
where the time goes:
time: 884 us; the launch traced here: 883 us
  waiting for transfers between devices  340 us (38%)
  blocking collectives  278 us (31%)
  local copies, waits for them, and re-layouts  212 us (24%)
  matrix products  27.8 us (3%)
  between operations  13.4 us (2%)
  other arithmetic  10.9 us (1%)
    psum x2, waiting for transfers between devices, per_device(): lax.psum(projected.astype(jnp.bfloat16), 'row').astype(jnp.float32)  292 us
    psum x1, blocking collectives, per_device(): squares = lax.psum(jnp.sum(slice_part * slice_part, axis=0), ('row', 'col'))  278 us
    scatter x1, local copies, waits for them, and re-layouts, per_device(): position = jnp.zeros((order_size,), jnp.int32).at[pole_order].set(jnp.ara...  120 us
    reduce_scatter x1, waiting for transfers between devices, per_device(): lax.psum_scatter(jnp.einsum('ck,rc->kr', mixing, old_block, preferred_ele...  28.4 us
    gather x1, local copies, waits for them, and re-layouts, per_device(): col_sq = pole_sq[sorted_pos]  23 us
    gather x1, local copies, waits for them, and re-layouts, per_device(): col_coupling = coupling[sorted_pos]  23 us
    gather x1, local copies, waits for them, and re-layouts, per_device(): col_live = (1 - deflated[sorted_pos]).astype(jnp.float32)  19.5 us
    all_gather x2, waiting for transfers between devices, per_device(): lax.all_gather(panel_rows, 'col', axis=1, tiled=True)  18.7 us
  transfers between devices with their start and end apart: 5, of which 4 were waited for; matrix products, arithmetic and copies ran while one was open for 27% of the time, Pallas kernels for 0%

commit v1 on v0

--- a/solution.py
+++ b/solution.py
@@ -2,6 +2,10 @@
 import jax.numpy as jnp
 from jax import lax
 from jax.sharding import PartitionSpec as P
+
+
+def _meet_rows(values, chip_axis):
+    return lax.all_gather(values, chip_axis).sum(axis=0)
 
 
 def secular_columns(col_sq, col_coupling, col_live, weight, anchor_sq, pole_gap, root_fraction):
@@ -80,7 +84,7 @@
             lax.all_gather(panel_rows, "col", axis=1, tiled=True),
             preferred_element_type=jnp.float32,
         )
-        projected = lax.psum(projected.astype(jnp.bfloat16), "row").astype(jnp.float32)
+        projected = _meet_rows(projected.astype(jnp.bfloat16), "row").astype(jnp.float32)
         coefficients = jnp.dot(projected, upper_tri[panel_index].T, precision=highest).astype(
             jnp.bfloat16
         )

time: 884 us -> 798 us (0.903)
  waiting for transfers between devices: 340 us -> 243 us
  other arithmetic: 10.9 us -> 20.4 us
    psum x2 -> x0, waiting for transfers between devices: 292 us -> none  [per_device(): lax.psum(projected.astype(jnp.bfloat16), 'row').astype(jnp.float32)]
    all_gather x0 -> x2, waiting for transfers between devices: none -> 199 us  [_meet_rows(): return lax.all_gather(values, chip_axis).sum(axis=0)]
    reduce_sum x0 -> x2, other arithmetic: none -> 9.51 us  [_meet_rows(): return lax.all_gather(values, chip_axis).sum(axis=0)]
  transfers between devices with their start and end apart: 5 -> 5, of which waited for: 4 -> 4; matrix products, arithmetic and copies ran while one was open for 27% -> 31% of each run, Pallas kernels for 0% -> 0%
where the time goes in v1:
time: 798 us; the launch traced here: 797 us
  blocking collectives  278 us (35%)
  waiting for transfers between devices  243 us (30%)
  local copies, waits for them, and re-layouts  216 us (27%)
  matrix products  25.9 us (3%)
  other arithmetic  20.4 us (3%)
  between operations  13.4 us (2%)
    psum x1, blocking collectives, per_device(): squares = lax.psum(jnp.sum(slice_part * slice_part, axis=0), ('row', 'col'))  278 us
    all_gather x2, waiting for transfers between devices, _meet_rows(): return lax.all_gather(values, chip_axis).sum(axis=0)  199 us
    scatter x1, local copies, waits for them, and re-layouts, per_device(): position = jnp.zeros((order_size,), jnp.int32).at[pole_order].set(jnp.ara...  120 us
    reduce_scatter x1, waiting for transfers between devices, per_device(): lax.psum_scatter(jnp.einsum('ck,rc->kr', mixing, old_block, preferred_ele...  28.4 us
    gather x1, local copies, waits for them, and re-layouts, per_device(): col_live = (1 - deflated[sorted_pos]).astype(jnp.float32)  23 us
    gather x1, local copies, waits for them, and re-layouts, per_device(): col_sq = pole_sq[sorted_pos]  23 us
    gather x1, local copies, waits for them, and re-layouts, per_device(): col_coupling = coupling[sorted_pos]  23 us
  transfers between devices with their start and end apart: 5, of which 4 were waited for; matrix products, arithmetic and copies ran while one was open for 31% of the time, Pallas kernels for 0%

profile of v1, /device:TPU:2, one launch (start us, length us, event | category | flops | bytes accessed | tf_op | source)
XLA Modules:
  0.0 797.3 jit_solution(17121134633861025609)
XLA Ops:
  6.5 0.0 copy-start
  6.5 0.0 all-gather.9.cloned.1.call-start
  6.5 1.9 fusion.23
  8.4 0.0 all-gather.9.cloned.1.call-update
  8.5 0.0 reduce-scatter.2.cloned.1.call-start
  8.5 0.9 compare_select_fusion
  9.5 120.1 %scatter_custom_fusion = s32[32768]{0:T(1024)S(1)} fusion(s32[32768]{0:T(1024)S(1)} %compare_select_fusion, s32[32768]{0:T(1024)S(1)} %iota.24, s32[]{:T(128)} %constant.25.clone.1), kind=kCustom, calls=%fused_computation.38 | custom fusion | bytes 131076 | tf_op jit(solution)/shard_map/scatter | solution.py:42
  129.6 0.0 copy-done.1
  129.6 23.0 %gather_fusion.2 = s32[4096]{0:T(1024)S(1)} fusion(s32[32768]{0:T(1024)S(1)} %copy-done.1, s32[4096]{0:T(1024)S(1)} %fusion.20), kind=kCustom, calls=%fused_computation.2 | custom fusion | bytes 49152 | tf_op jit(solution)/shard_map/gather | solution.py:47
  152.7 0.0 copy-done
  152.7 0.0 copy-start.4
  152.7 23.0 %gather_fusion.4 = f32[4096]{0:T(1024)S(1)} fusion(f32[32768]{0:T(1024)S(1)} %copy-done, s32[4096]{0:T(1024)S(1)} %fusion.20), kind=kCustom, calls=%fused_computation.4 | custom fusion | bytes 49152 | tf_op jit(solution)/shard_map/gather | solution.py:45
  175.7 0.0 copy-done.4
  175.7 0.0 copy-start.3
  175.7 0.0 copy-start.2
  175.8 6.2 gather_fusion.5
  181.9 6.2 gather_fusion
  188.1 0.0 copy-done.3
  188.1 6.2 gather_fusion.1
  194.3 0.0 copy-start.5
  194.3 23.0 %gather_fusion.3 = f32[4096]{0:T(1024)S(1)} fusion(f32[32768]{0:T(1024)S(1)} %copy-done.2, s32[4096]{0:T(1024)S(1)} %fusion.20), kind=kCustom, calls=%fused_computation.3 | custom fusion | bytes 49152 | tf_op jit(solution)/shard_map/gather | solution.py:46
  217.3 6.2 gather_fusion.6
  223.5 6.5 subtract_divide_fusion
  230.0 1.3 multiply_reduce_fusion
  231.3 278.5 %psum.7 = f32[1024]{0:T(1024)S(1)} all-reduce(f32[1024]{0:T(1024)S(1)} %multiply_reduce_fusion), channel_id=1, replica_groups=mesh['side'=2,'row'=32,'col'=4] {'row','col'}, use_global_device_ids=true, to_apply=%region_3.4 | all-reduce | flops 1024 | bytes 8192 | tf_op jit(solution)/shard_map/psum | solution.py:62
  509.8 15.3 %fusion.5 = bf16[1024,1024]{1,0:T(8,128)(2,1)} fusion(bf16[1,1024,4096]{2,1,0:T(8,128)(2,1)} %param.9, s32[1024]{0:T(1024)S(1)} %gather_fusion.1, s32[4096]{0:T(1024)S(1)} %iota_add_fusion, pred[1024]{0:T(1024)(128)(4,1)S(1)} %get-tuple-element.6, f32[1024]{0:T(1024)S(1)} %subtract_multiply_fusion, f32[1024]{0:T(1024)S(1)} %gather_fusion.5, ...), kind=kOutput, calls=%fused_computation.16 | convolution fusion | flops 8620343296 | bytes 10548224 | tf_op jit(solution)/shard_map/ck,rc->kr/dot_general | solution.py:65
  525.2 0.0 reduce-scatter.2.cloned.1.call-update
  525.2 0.0 all-gather.11.cloned.1.call-start
  525.3 0.1 dynamic_slice.11
  525.3 28.4 %reduce-scatter.2.cloned.1.call-done = bf16[256,1024]{1,0:T(8,128)(2,1)} async-done(((bf16[1024,1024]{1,0:T(8,128)(2,1)}), bf16[256,1024]{1,0:T(8,128)(2,1)}) %reduce-scatter.2.cloned.1.call-update) | async-done | bytes 524304 | tf_op jit(solution)/shard_map/reduce_scatter | solution.py:64
  553.8 2.6 convolution_convert_fusion.3
  556.4 0.0 all-gather.11.cloned.1.call-update
  556.4 0.0 all-gather.13.cloned.1.call-start
  556.4 0.5 all-gather.13.cloned.1.call-update
  557.0 0.3 all-gather.15.cloned.1.call-start
  557.2 0.2 iota_compare_fusion
  557.5 2.0 bitcast_select_fusion
  559.4 98.5 %all-gather.11.cloned.1.call-done = bf16[8192,512]{1,0:T(8,128)(2,1)} async-done(((bf16[256,512]{1,0:T(8,128)(2,1)}), bf16[8192,512]{1,0:T(8,128)(2,1)}) %all-gather.11.cloned.1.call-update) | async-done | bytes 8388624 | tf_op jit(solution)/shard_map/all_gather | solution.py:8
  657.9 4.8 reduce_sum.34
  662.7 0.7 convolution_convert_fusion.2
  663.4 1.8 convolution_subtract_fusion.1
  665.2 14.9 %all-gather.13.cloned.1.call-done = bf16[1,1,1024,512]{3,2,1,0:T(8,128)(2,1)} async-done(((bf16[1,1,1024,128]{3,2,1,0:T(8,128)(2,1)}), bf16[1,1,1024,512]{3,2,1,0:T(8,128)(2,1)}) %all-gather.13.cloned.1.call-update) | async-done | bytes 1048592 | tf_op jit(solution)/shard_map/all_gather | solution.py:84
  680.2 2.4 convolution_convert_fusion.1
  682.5 0.0 all-gather.15.cloned.1.call-update
  682.6 100.3 %all-gather.15.cloned.1.call-done = bf16[8192,512]{1,0:T(8,128)(2,1)} async-done(((bf16[256,512]{1,0:T(8,128)(2,1)}), bf16[8192,512]{1,0:T(8,128)(2,1)}) %all-gather.15.cloned.1.call-update) | async-done | bytes 8388624 | tf_op jit(solution)/shard_map/all_gather | solution.py:8
  782.9 4.8 reduce_sum.35
  787.6 0.7 convolution_convert_fusion
  788.3 2.5 fusion.9
  (12 shorter events, 0.1 us)
Async XLA Ops:
  6.5 146.1 %copy-start = (f32[32768]{0:T(1024)S(1)}, f32[32768]{0:T(1024)}, u32[]{:S(2)}) copy-start(f32[32768]{0:T(1024)} %param.12) | copy-start | bytes 393220
  6.5 123.1 %copy-start.1 = (s32[32768]{0:T(1024)S(1)}, s32[32768]{0:T(1024)}, u32[]{:S(2)}) copy-start(s32[32768]{0:T(1024)} %param.14) | copy-start | bytes 393220
  6.5 518.8 %all-gather.9.cloned.1.call-start = ((), (), s32[]{:S(2)}) async-start(), calls=%async_computation.2 | async-start | bytes 1310720 | tf_op jit(solution)/shard_map/all_gather | solution.py:84
  8.5 545.3 %reduce-scatter.2.cloned.1.call-start = ((), (), s32[]{:S(2)}) async-start(), calls=%async_computation.1 | async-start | bytes 2621440 | tf_op jit(solution)/shard_map/reduce_scatter | solution.py:64
  152.7 23.1 %copy-start.4 = (s32[1024]{0:T(1024)S(1)}, s32[1024]{0:T(1024)}, u32[]{:S(2)}) copy-start(s32[1024]{0:T(1024)} %param.16) | copy-start | bytes 12292
  175.7 12.4 %copy-start.3 = (s32[32768]{0:T(1024)S(1)}, s32[32768]{0:T(1024)}, u32[]{:S(2)}) copy-start(s32[32768]{0:T(1024)} %param.15) | copy-start | bytes 393220
  175.7 18.5 %copy-start.2 = (f32[32768]{0:T(1024)S(1)}, f32[32768]{0:T(1024)}, u32[]{:S(2)}) copy-start(f32[32768]{0:T(1024)} %param.13) | copy-start | bytes 393220
  194.3 29.2 %copy-start.5 = (f32[1024]{0:T(1024)S(1)}, f32[1024]{0:T(1024)}, u32[]{:S(2)}) copy-start(f32[1024]{0:T(1024)} %param.17) | copy-start | bytes 12292
  525.2 132.7 %all-gather.11.cloned.1.call-start = ((), (), s32[]{:S(2)}) async-start(), calls=%async_computation.3 | async-start | bytes 8650752 | tf_op jit(solution)/shard_map/all_gather | solution.py:8
  556.4 123.8 %all-gather.13.cloned.1.call-start = ((), (), s32[]{:S(2)}) async-start(), calls=%async_computation.4 | async-start | bytes 1310720 | tf_op jit(solution)/shard_map/all_gather | solution.py:84
  557.0 225.9 %all-gather.15.cloned.1.call-start = ((), (), s32[]{:S(2)}) async-start(), calls=%async_computation.5 | async-start | bytes 8650752 | tf_op jit(solution)/shard_map/all_gather | solution.py:8
Sparse Core Ops, SparseCore 0:
  9.2 26.2 all-gather.8
  525.3 28.4 reduce-scatter.1
  556.7 101.1 all-gather.10
  659.7 20.3 all-gather.12
  682.9 99.8 all-gather.14
